TPU v7x, 32 devices: a whole 2x2x4 slice. The times are simulated.
32 devices in a mesh: parts: 2 (over y), leaf: 4 (over z), top: 4 (over x, core).
Axes of the slice: x: 2, y: 2, z: 4, core: 2. Of those that a mesh axis runs over, the one named last changes fastest.
Arguments:
- right_side: float32 [8, 2560, 256], P(('parts', 'top'), 'leaf'), parts along dimension 0, may hold values from -6 to 6
- leaf_inverse: bfloat16 [8, 2560, 640], P(('parts', 'top'), 'leaf'), parts along dimension 0, as said below
- left_basis: bfloat16 [2, 8, 2560, 128], P(None, ('parts', 'top'), 'leaf'), parts along dimension 1, may hold values from -0.1875 to 0.1875
- right_basis: bfloat16 [2, 8, 2560, 128], P(None, ('parts', 'top'), 'leaf'), parts along dimension 1, may hold values from -6 to 6
- level_caps: bfloat16 [2, 8, 512, 256], P(None, ('parts', 'top'), 'leaf'), parts along dimension 1, may hold values from -0.375 to 0.375
- top_left: bfloat16 [8, 2560, 128], P(('parts', 'top'), 'leaf'), parts along dimension 0, may hold values from -0.1875 to 0.1875
- top_right: bfloat16 [8, 2560, 128], P(('parts', 'top'), 'leaf'), parts along dimension 0, may hold values from -6 to 6
- top_caps: bfloat16 [1024, 512], P(('parts', 'top')), parts along dimension 0, may hold values from -0.25 to 0.25
Outputs:
- solution: float32 [8, 2560, 256], P(('parts', 'top'), 'leaf'), parts along dimension 0
There are 2 independent parts, one for each index of `parts`. A program takes and returns all parts, laid end to end along the dimension named above; each array names one. Nothing has to cross between parts.
Inputs may be any that keep to these rules, and one draw needn't show every extreme that they name: Each leaf block of leaf_inverse is lower triangular with a positive diagonal.
All inputs are finite; a program needn't handle non-finite values.
Results may differ from a plain program's by a relative error of at most 0.0075.
Values may be sent and summed in bfloat16 or wider, within the bound.
No kernel may reach another device: no remote copies, remote signals or barrier semaphores. Data moves between devices by JAX's collectives and lax.ppermute only.
A program may use at most 64 MiB of HBM per device.

v0:
```python
import math
import jax
import jax.numpy as jnp
from jax import lax
from jax.sharding import PartitionSpec as P


def from_partner(value, axis, distance):
    mask = 2**distance
    pairs = [(source, source ^ mask) for source in range(lax.axis_size(axis))]
    return lax.ppermute(value, axis, pairs)


def project_rows(basis, current):
    return lax.dot_general(
        basis,
        current.astype(jnp.bfloat16),
        (((0,), (0,)), ((), ())),
        preferred_element_type=jnp.float32,
    )


def pair_swaps(partial_value, shift_bits):
    position = lax.axis_index("leaf") >> shift_bits
    for bit_index in range(shift_bits):
        partial_value = partial_value + from_partner(partial_value, "leaf", bit_index)
    sibling_sum = from_partner(partial_value.astype(jnp.bfloat16), "leaf", shift_bits).astype(
        partial_value.dtype
    )
    lower_side = position & 1 == 0
    return jnp.where(
        lower_side,
        jnp.concatenate([partial_value, sibling_sum], 0),
        jnp.concatenate([sibling_sum, partial_value], 0),
    )


def level_update(current, project_basis, update_basis, caps_rows, level_num):
    leaf_rows = current.shape[0]
    shift_bits = level_num - 1
    partial_value = project_rows(project_basis, current) * (
        1.0 / math.sqrt(leaf_rows * 2**shift_bits)
    )
    stacked = pair_swaps(partial_value, shift_bits)
    weights = jnp.dot(
        caps_rows, stacked.astype(jnp.bfloat16), preferred_element_type=jnp.float32
    ).astype(jnp.bfloat16)
    return current - jnp.dot(update_basis, weights, preferred_element_type=jnp.float32)


def top_update(current, project_basis, update_basis, caps_rows):
    leaf_count = lax.axis_size("leaf")
    partial_value = project_rows(project_basis, current) * (
        1.0 / math.sqrt(leaf_count * current.shape[0])
    )
    column_total = lax.psum(partial_value, "leaf")
    stacked = lax.all_gather(column_total.astype(jnp.bfloat16), "top", axis=0, tiled=True)
    weights = jnp.dot(caps_rows, stacked, preferred_element_type=jnp.float32).astype(jnp.bfloat16)
    return current - jnp.dot(update_basis, weights, preferred_element_type=jnp.float32)


def on_device(
    right_side, leaf_inverse, left_basis, right_basis, level_caps, top_left, top_right, top_caps
):
    levels = left_basis.shape[0]
    inverse_block = leaf_inverse[0]
    current = jnp.dot(
        inverse_block, right_side[0].astype(jnp.bfloat16), preferred_element_type=jnp.float32
    )
    for level_num in range(1, levels + 1):
        current = level_update(
            current,
            right_basis[level_num - 1, 0],
            left_basis[level_num - 1, 0],
            level_caps[level_num - 1, 0],
            level_num,
        )
    current = top_update(current, top_right[0], top_left[0], top_caps)
    current = top_update(current, top_left[0], top_right[0], top_caps)
    for level_num in range(levels, 0, -1):
        current = level_update(
            current,
            left_basis[level_num - 1, 0],
            right_basis[level_num - 1, 0],
            level_caps[level_num - 1, 0],
            level_num,
        )
    current = project_rows(inverse_block, current)
    return current[None]


def solution(mesh):
    return jax.shard_map(
        on_device,
        mesh=mesh,
        in_specs=(
            P(("parts", "top"), "leaf", None),
            P(("parts", "top"), "leaf", None),
            P(None, ("parts", "top"), "leaf", None),
            P(None, ("parts", "top"), "leaf", None),
            P(None, ("parts", "top"), "leaf", None),
            P(("parts", "top"), "leaf", None),
            P(("parts", "top"), "leaf", None),
            P(("parts", "top"), None),
        ),
        out_specs=P(("parts", "top"), "leaf", None),
        check_vma=False,
    )
```

profile of v0, /device:TPU:0, one launch (start us, length us, event | category | flops | bytes accessed | tf_op | source)
XLA Modules:
  0.0 93.3 jit_solution(5820424412641615513)
XLA Ops:
  0.0 1.1 %copy-done = bf16[1,640,640]{2,1,0:T(8,128)(2,1)S(1)} copy-done((bf16[1,640,640]{2,1,0:T(8,128)(2,1)S(1)}, bf16[1,640,640]{2,1,0:T(8,128)(2,1)}, u32[]{:S(2)}) %copy-start) | copy-done | bytes 819224
  1.1 1.5 %fusion.14 = f32[640,256]{1,0:T(8,128)S(1)} fusion(bf16[1,640,640]{2,1,0:T(8,128)(2,1)S(1)} %copy-done, f32[1,640,256]{2,1,0:T(8,128)} %param.8), kind=kOutput, calls=%fused_computation.33 | convolution fusion | flops 209879040 | bytes 2129920 | tf_op jit(solution)/shard_map/dot_general | solution.py:67
  3.0 3.1 %collective-permute-start = (bf16[128,256]{1,0:T(8,128)(2,1)S(1)}, bf16[128,256]{1,0:T(8,128)(2,1)S(1)}, u32[]{:S(2)}, u32[]{:S(2)}) collective-permute-start(bf16[128,256]{1,0:T(8,128)(2,1)S(1)} %fusion.12), channel_id=1, source_target_pairs={{0,4},{4,0},{8,12},{12,8},{1,5},{5,1},{9,13},{13,9},{2,6},{6,2},{1... | collective-permute-start | bytes 196616 | tf_op jit(solution)/shard_map/ppermute | solution.py:11
  6.1 2.2 %collective-permute-done = bf16[128,256]{1,0:T(8,128)(2,1)S(1)} collective-permute-done((bf16[128,256]{1,0:T(8,128)(2,1)S(1)}, bf16[128,256]{1,0:T(8,128)(2,1)S(1)}, u32[]{:S(2)}, u32[]{:S(2)}) %collective-permute-start) | collective-permute-done | bytes 65568 | tf_op jit(solution)/shard_map/ppermute | solution.py:11
  8.3 0.5 fusion.5
  9.1 2.1 %collective-permute-start.1 = (f32[128,256]{1,0:T(8,128)S(1)}, f32[128,256]{1,0:T(8,128)S(1)}, u32[]{:S(2)}, u32[]{:S(2)}) collective-permute-start(f32[128,256]{1,0:T(8,128)S(1)} %fusion.11), channel_id=1, source_target_pairs={{0,4},{4,0},{8,12},{12,8},{1,5},{5,1},{9,13},{13,9},{2,6},{6,2},{1... | collective-permute-start | bytes 393224 | tf_op jit(solution)/shard_map/ppermute | solution.py:11
  11.1 3.0 %collective-permute-done.1 = f32[128,256]{1,0:T(8,128)S(1)} collective-permute-done((f32[128,256]{1,0:T(8,128)S(1)}, f32[128,256]{1,0:T(8,128)S(1)}, u32[]{:S(2)}, u32[]{:S(2)}) %collective-permute-start.1) | collective-permute-done | bytes 131104 | tf_op jit(solution)/shard_map/ppermute | solution.py:11
  14.1 3.1 %collective-permute-start.2 = (bf16[128,256]{1,0:T(8,128)(2,1)S(1)}, bf16[128,256]{1,0:T(8,128)(2,1)S(1)}, u32[]{:S(2)}, u32[]{:S(2)}) collective-permute-start(bf16[128,256]{1,0:T(8,128)(2,1)S(1)} %add.10), channel_id=1, source_target_pairs={{0,8},{4,12},{8,0},{12,4},{1,9},{5,13},{9,1},{13,5},{2,10},{6,14},... | collective-permute-start | bytes 196616 | tf_op jit(solution)/shard_map/ppermute | solution.py:11
  17.2 2.2 %collective-permute-done.2 = bf16[128,256]{1,0:T(8,128)(2,1)S(1)} collective-permute-done((bf16[128,256]{1,0:T(8,128)(2,1)S(1)}, bf16[128,256]{1,0:T(8,128)(2,1)S(1)}, u32[]{:S(2)}, u32[]{:S(2)}) %collective-permute-start.2) | collective-permute-done | bytes 65568 | tf_op jit(solution)/shard_map/ppermute | solution.py:11
  19.5 0.5 fusion.4
  20.3 22.1 %all-reduce.2 = bf16[128,256]{0,1:T(8,128)(2,1)S(1)} all-reduce(f32[128,256]{0,1:T(8,128)S(1)} %fusion.10), channel_id=1, replica_groups=mesh['parts'=2,'leaf'=4,'top'=4] {'leaf'}, use_global_device_ids=true, to_apply=%region_0.1 | all-reduce | flops 32768 | bytes 196608 | tf_op jit(solution)/shard_map/psum | solution.py:56
  42.4 5.9 %all_gather.6 = bf16[512,256]{0,1:T(8,128)(2,1)S(1)} all-gather(bf16[128,256]{0,1:T(8,128)(2,1)S(1)} %all-reduce.2), channel_id=1, replica_groups=mesh['parts'=2,'leaf'=4,'top'=4] {'top'}, dimensions={0}, use_global_device_ids=true | all-gather | bytes 327680 | tf_op jit(solution)/shard_map/all_gather | solution.py:57
  48.3 0.6 fusion.3
  48.9 0.3 fusion.9
  49.2 18.4 %all-reduce.3 = bf16[128,256]{0,1:T(8,128)(2,1)S(1)} all-reduce(f32[128,256]{0,1:T(8,128)S(1)} %fusion.9), channel_id=1, replica_groups=mesh['parts'=2,'leaf'=4,'top'=4] {'leaf'}, use_global_device_ids=true, to_apply=%region_1.2 | all-reduce | flops 32768 | bytes 196608 | tf_op jit(solution)/shard_map/psum | solution.py:56
  67.7 5.9 %all_gather.7 = bf16[512,256]{0,1:T(8,128)(2,1)S(1)} all-gather(bf16[128,256]{0,1:T(8,128)(2,1)S(1)} %all-reduce.3), channel_id=1, replica_groups=mesh['parts'=2,'leaf'=4,'top'=4] {'top'}, dimensions={0}, use_global_device_ids=true | all-gather | bytes 327680 | tf_op jit(solution)/shard_map/all_gather | solution.py:57
  73.6 0.6 fusion.2
  74.6 5.7 %collective-permute-done.3 = f32[128,256]{1,0:T(8,128)S(1)} collective-permute-done((f32[128,256]{1,0:T(8,128)S(1)}, f32[128,256]{1,0:T(8,128)S(1)}, u32[]{:S(2)}, u32[]{:S(2)}) %collective-permute-start.3) | collective-permute-done | bytes 131104 | tf_op jit(solution)/shard_map/ppermute | solution.py:11
  80.3 0.8 collective-permute-start.4
  81.1 5.1 %collective-permute-done.4 = bf16[128,256]{1,0:T(8,128)(2,1)S(1)} collective-permute-done((bf16[128,256]{1,0:T(8,128)(2,1)S(1)}, bf16[128,256]{1,0:T(8,128)(2,1)S(1)}, u32[]{:S(2)}, u32[]{:S(2)}) %collective-permute-start.4) | collective-permute-done | bytes 65568 | tf_op jit(solution)/shard_map/ppermute | solution.py:11
  86.2 0.5 fusion.1
  87.0 4.3 %collective-permute-done.5 = bf16[128,256]{1,0:T(8,128)(2,1)S(1)} collective-permute-done((bf16[128,256]{1,0:T(8,128)(2,1)S(1)}, bf16[128,256]{1,0:T(8,128)(2,1)S(1)}, u32[]{:S(2)}, u32[]{:S(2)}) %collective-permute-start.5) | collective-permute-done | bytes 65568 | tf_op jit(solution)/shard_map/ppermute | solution.py:11
  91.5 0.8 convolution_bitcast_fusion
  92.3 1.1 %copy.14 = f32[1,640,256]{2,1,0:T(8,128)} copy(f32[1,640,256]{1,2,0:T(8,128)S(1)} %convolution_bitcast_fusion) | data formatting | bytes 1310720 | tf_op jit(solution)/shard_map/broadcast_in_dim | solution.py:89
  (29 shorter events, 1.8 us)
Async XLA Ops:
  0.0 1.1 %copy-start = (bf16[1,640,640]{2,1,0:T(8,128)(2,1)S(1)}, bf16[1,640,640]{2,1,0:T(8,128)(2,1)}, u32[]{:S(2)}) copy-start(bf16[1,640,640]{2,1,0:T(8,128)(2,1)} %param.9) | copy-start | bytes 2457604
  0.0 2.7 %copy-start.1 = (bf16[2,1,640,128]{3,2,1,0:T(8,128)(2,1)S(1)}, bf16[2,1,640,128]{3,2,1,0:T(8,128)(2,1)}, u32[]{:S(2)}) copy-start(bf16[2,1,640,128]{3,2,1,0:T(8,128)(2,1)} %param.11) | copy-start | bytes 983044
  2.7 5.6 %copy-start.2 = (bf16[2,1,640,128]{3,2,1,0:T(8,128)(2,1)S(1)}, bf16[2,1,640,128]{3,2,1,0:T(8,128)(2,1)}, u32[]{:S(2)}) copy-start(bf16[2,1,640,128]{3,2,1,0:T(8,128)(2,1)} %param.10) | copy-start | bytes 983044
  2.7 5.6 %copy-start.8 = (bf16[2,1,128,256]{3,2,1,0:T(8,128)(2,1)S(1)}, bf16[2,1,128,256]{3,2,1,0:T(8,128)(2,1)}, u32[]{:S(2)}) copy-start(bf16[2,1,128,256]{3,2,1,0:T(8,128)(2,1)} %param.12) | copy-start | bytes 393220
  3.0 5.3 %collective-permute-start = (bf16[128,256]{1,0:T(8,128)(2,1)S(1)}, bf16[128,256]{1,0:T(8,128)(2,1)S(1)}, u32[]{:S(2)}, u32[]{:S(2)}) collective-permute-start(bf16[128,256]{1,0:T(8,128)(2,1)S(1)} %fusion.12), channel_id=1, source_target_pairs={{0,4},{4,0},{8,12},{12,8},{1,5},{5,1},{9,13},{13,9},{2,6},{6,2},{1... | collective-permute-start | bytes 196616 | tf_op jit(solution)/shard_map/ppermute | solution.py:11
  9.1 5.0 %collective-permute-start.1 = (f32[128,256]{1,0:T(8,128)S(1)}, f32[128,256]{1,0:T(8,128)S(1)}, u32[]{:S(2)}, u32[]{:S(2)}) collective-permute-start(f32[128,256]{1,0:T(8,128)S(1)} %fusion.11), channel_id=1, source_target_pairs={{0,4},{4,0},{8,12},{12,8},{1,5},{5,1},{9,13},{13,9},{2,6},{6,2},{1... | collective-permute-start | bytes 393224 | tf_op jit(solution)/shard_map/ppermute | solution.py:11
  14.1 5.3 %collective-permute-start.2 = (bf16[128,256]{1,0:T(8,128)(2,1)S(1)}, bf16[128,256]{1,0:T(8,128)(2,1)S(1)}, u32[]{:S(2)}, u32[]{:S(2)}) collective-permute-start(bf16[128,256]{1,0:T(8,128)(2,1)S(1)} %add.10), channel_id=1, source_target_pairs={{0,8},{4,12},{8,0},{12,4},{1,9},{5,13},{9,1},{13,5},{2,10},{6,14},... | collective-permute-start | bytes 196616 | tf_op jit(solution)/shard_map/ppermute | solution.py:11
  17.2 2.7 %copy-start.4 = (bf16[1,640,128]{2,1,0:T(8,128)(2,1)S(1)}, bf16[1,640,128]{2,1,0:T(8,128)(2,1)}, u32[]{:S(2)}) copy-start(bf16[1,640,128]{2,1,0:T(8,128)(2,1)} %param.14) | copy-start | bytes 491524
  42.4 6.0 %copy-start.3 = (bf16[1,640,128]{2,1,0:T(8,128)(2,1)S(1)}, bf16[1,640,128]{2,1,0:T(8,128)(2,1)}, u32[]{:S(2)}) copy-start(bf16[1,640,128]{2,1,0:T(8,128)(2,1)} %param.13) | copy-start | bytes 491524
  42.4 6.0 %copy-start.6 = (bf16[128,512]{1,0:T(8,128)(2,1)S(1)}, bf16[128,512]{1,0:T(8,128)(2,1)}, u32[]{:S(2)}) copy-start(bf16[128,512]{1,0:T(8,128)(2,1)} %param.15) | copy-start | bytes 393220
  67.7 6.0 %copy-start.5 = (bf16[1,640,128]{2,1,0:T(8,128)(2,1)S(1)}, bf16[1,640,128]{2,1,0:T(8,128)(2,1)}, u32[]{:S(2)}) copy-start(bf16[1,640,128]{2,1,0:T(8,128)(2,1)} %param.14) | copy-start | bytes 491524
  67.7 6.0 %copy-start.7 = (bf16[128,512]{1,0:T(8,128)(2,1)S(1)}, bf16[128,512]{1,0:T(8,128)(2,1)}, u32[]{:S(2)}) copy-start(bf16[128,512]{1,0:T(8,128)(2,1)} %param.15) | copy-start | bytes 393220
  74.5 11.7 %copy-start.9 = (bf16[2,1,128,256]{3,2,1,0:T(8,128)(2,1)S(1)}, bf16[2,1,128,256]{3,2,1,0:T(8,128)(2,1)}, u32[]{:S(2)}) copy-start(bf16[2,1,128,256]{3,2,1,0:T(8,128)(2,1)} %param.12) | copy-start | bytes 393220
  74.5 5.8 %collective-permute-start.3 = (f32[128,256]{1,0:T(8,128)S(1)}, f32[128,256]{1,0:T(8,128)S(1)}, u32[]{:S(2)}, u32[]{:S(2)}) collective-permute-start(f32[128,256]{1,0:T(8,128)S(1)} %fusion.8), channel_id=1, source_target_pairs={{0,4},{4,0},{8,12},{12,8},{1,5},{5,1},{9,13},{13,9},{2,6},{6,2},{1... | collective-permute-start | bytes 393224 | tf_op jit(solution)/shard_map/ppermute | solution.py:11
  80.3 5.9 %collective-permute-start.4 = (bf16[128,256]{1,0:T(8,128)(2,1)S(1)}, bf16[128,256]{1,0:T(8,128)(2,1)S(1)}, u32[]{:S(2)}, u32[]{:S(2)}) collective-permute-start(bf16[128,256]{1,0:T(8,128)(2,1)S(1)} %add.11), channel_id=1, source_target_pairs={{0,8},{4,12},{8,0},{12,4},{1,9},{5,13},{9,1},{13,5},{2,10},{6,14},... | collective-permute-start | bytes 196616 | tf_op jit(solution)/shard_map/ppermute | solution.py:11
  86.9 4.3 %collective-permute-start.5 = (bf16[128,256]{1,0:T(8,128)(2,1)S(1)}, bf16[128,256]{1,0:T(8,128)(2,1)S(1)}, u32[]{:S(2)}, u32[]{:S(2)}) collective-permute-start(bf16[128,256]{1,0:T(8,128)(2,1)S(1)} %fusion.7), channel_id=1, source_target_pairs={{0,4},{4,0},{8,12},{12,8},{1,5},{5,1},{9,13},{13,9},{2,6},{6,2},{1... | collective-permute-start | bytes 196616 | tf_op jit(solution)/shard_map/ppermute | solution.py:11
where the time goes:
time: 93.6 us; the launch traced here: 93.3 us
  blocking collectives  52.4 us (56%)
  waiting for transfers between devices  22.5 us (24%)
  starting transfers between devices  9.21 us (10%)
  matrix products  6.72 us (7%)
  local copies, waits for them, and re-layouts  2.27 us (2%)
    psum x2, blocking collectives, top_update(): column_total = lax.psum(partial_value, 'leaf')  40.5 us
    ppermute x6, waiting for transfers between devices, from_partner(): return lax.ppermute(value, axis, pairs)  22.5 us
    all_gather x2, blocking collectives, top_update(): lax.all_gather(column_total.astype(jnp.bfloat16), 'top', axis=0, tiled=True)  11.9 us
    ppermute x6, starting transfers between devices, from_partner(): return lax.ppermute(value, axis, pairs)  9.21 us
    dot_general x7, matrix products, project_rows(): lax.dot_general(basis, current.astype(jnp.bfloat16), (((0,), (0,)), ((),...  2.41 us
  transfers between devices with their start and end apart: 6, of which 6 were waited for; matrix products, arithmetic and copies ran while one was open for 0% of the time, Pallas kernels for 0%

commit v1 on v0

--- a/solution.py
+++ b/solution.py
@@ -3,6 +3,8 @@
 import jax.numpy as jnp
 from jax import lax
 from jax.sharding import PartitionSpec as P
+
+islands_expand = lambda content, peer_axis: jnp.sum(lax.all_gather(content, axis_name=peer_axis), 0)
 
 
 def from_partner(value, axis, distance):
@@ -53,7 +55,7 @@
     partial_value = project_rows(project_basis, current) * (
         1.0 / math.sqrt(leaf_count * current.shape[0])
     )
-    column_total = lax.psum(partial_value, "leaf")
+    column_total = islands_expand(partial_value, "leaf")
     stacked = lax.all_gather(column_total.astype(jnp.bfloat16), "top", axis=0, tiled=True)
     weights = jnp.dot(caps_rows, stacked, preferred_element_type=jnp.float32).astype(jnp.bfloat16)
     return current - jnp.dot(update_basis, weights, preferred_element_type=jnp.float32)

time: 93.6 us -> 86.1 us (0.920)
  blocking collectives: 52.4 us -> 44.4 us
  waiting for transfers between devices: 22.5 us -> 17.8 us
  starting transfers between devices: 9.21 us -> 13.5 us
    psum x2 -> x0, blocking collectives: 40.5 us -> none  [top_update(): column_total = lax.psum(partial_value, 'leaf')]
    all_gather x0 -> x2, blocking collectives: none -> 32.5 us  [lax.all_gather(content, axis_name=peer_axis)]
    ppermute x6, waiting for transfers between devices: 22.5 us -> 17.8 us  [from_partner(): return lax.ppermute(value, axis, pairs)]
    ppermute x6, starting transfers between devices: 9.21 us -> 13.5 us  [from_partner(): return lax.ppermute(value, axis, pairs)]
where the time goes in v1:
time: 86.1 us; the launch traced here: 85.9 us
  blocking collectives  44.4 us (52%)
  waiting for transfers between devices  17.8 us (21%)
  starting transfers between devices  13.5 us (16%)
  matrix products  6.7 us (8%)
  local copies, waits for them, and re-layouts  2.63 us (3%)
    all_gather x2, blocking collectives, lax.all_gather(content, axis_name=peer_axis)  32.5 us
    ppermute x6, waiting for transfers between devices, from_partner(): return lax.ppermute(value, axis, pairs)  17.8 us
    ppermute x6, starting transfers between devices, from_partner(): return lax.ppermute(value, axis, pairs)  13.5 us
    all_gather x2, blocking collectives, top_update(): lax.all_gather(column_total.astype(jnp.bfloat16), 'top', axis=0, tiled=True)  11.9 us
    dot_general x7, matrix products, project_rows(): lax.dot_general(basis, current.astype(jnp.bfloat16), (((0,), (0,)), ((),...  2.39 us
  transfers between devices with their start and end apart: 6, of which 6 were waited for; matrix products, arithmetic and copies ran while one was open for 0% of the time, Pallas kernels for 0%

profile of v1, /device:TPU:0, one launch (start us, length us, event | category | flops | bytes accessed | tf_op | source)
XLA Modules:
  0.0 85.9 jit_solution(6157185643568716368)
XLA Ops:
  0.0 1.1 %copy-done = bf16[1,640,640]{2,1,0:T(8,128)(2,1)S(1)} copy-done((bf16[1,640,640]{2,1,0:T(8,128)(2,1)S(1)}, bf16[1,640,640]{2,1,0:T(8,128)(2,1)}, u32[]{:S(2)}) %copy-start) | copy-done | bytes 819224
  1.1 1.5 %fusion.14 = f32[640,256]{1,0:T(8,128)S(1)} fusion(bf16[1,640,640]{2,1,0:T(8,128)(2,1)S(1)} %copy-done, f32[1,640,256]{2,1,0:T(8,128)} %param.8), kind=kOutput, calls=%fused_computation.33 | convolution fusion | flops 209879040 | bytes 2129920 | tf_op jit(solution)/shard_map/dot_general | solution.py:69
  3.0 3.1 %collective-permute-start = (bf16[128,256]{1,0:T(8,128)(2,1)S(1)}, bf16[128,256]{1,0:T(8,128)(2,1)S(1)}, u32[]{:S(2)}, u32[]{:S(2)}) collective-permute-start(bf16[128,256]{1,0:T(8,128)(2,1)S(1)} %fusion.12), channel_id=1, source_target_pairs={{0,4},{4,0},{8,12},{12,8},{1,5},{5,1},{9,13},{13,9},{2,6},{6,2},{1... | collective-permute-start | bytes 196616 | tf_op jit(solution)/shard_map/ppermute | solution.py:13
  6.1 2.2 %collective-permute-done = bf16[128,256]{1,0:T(8,128)(2,1)S(1)} collective-permute-done((bf16[128,256]{1,0:T(8,128)(2,1)S(1)}, bf16[128,256]{1,0:T(8,128)(2,1)S(1)}, u32[]{:S(2)}, u32[]{:S(2)}) %collective-permute-start) | collective-permute-done | bytes 65568 | tf_op jit(solution)/shard_map/ppermute | solution.py:13
  9.1 2.1 %collective-permute-start.1 = (f32[128,256]{1,0:T(8,128)S(1)}, f32[128,256]{1,0:T(8,128)S(1)}, u32[]{:S(2)}, u32[]{:S(2)}) collective-permute-start(f32[128,256]{1,0:T(8,128)S(1)} %fusion.11), channel_id=1, source_target_pairs={{0,4},{4,0},{8,12},{12,8},{1,5},{5,1},{9,13},{13,9},{2,6},{6,2},{1... | collective-permute-start | bytes 393224 | tf_op jit(solution)/shard_map/ppermute | solution.py:13
  11.1 3.0 %collective-permute-done.1 = f32[128,256]{1,0:T(8,128)S(1)} collective-permute-done((f32[128,256]{1,0:T(8,128)S(1)}, f32[128,256]{1,0:T(8,128)S(1)}, u32[]{:S(2)}, u32[]{:S(2)}) %collective-permute-start.1) | collective-permute-done | bytes 131104 | tf_op jit(solution)/shard_map/ppermute | solution.py:13
  14.1 3.1 %collective-permute-start.2 = (bf16[128,256]{1,0:T(8,128)(2,1)S(1)}, bf16[128,256]{1,0:T(8,128)(2,1)S(1)}, u32[]{:S(2)}, u32[]{:S(2)}) collective-permute-start(bf16[128,256]{1,0:T(8,128)(2,1)S(1)} %add.6), channel_id=1, source_target_pairs={{0,8},{4,12},{8,0},{12,4},{1,9},{5,13},{9,1},{13,5},{2,10},{6,14},... | collective-permute-start | bytes 196616 | tf_op jit(solution)/shard_map/ppermute | solution.py:13
  17.2 2.2 %collective-permute-done.2 = bf16[128,256]{1,0:T(8,128)(2,1)S(1)} collective-permute-done((bf16[128,256]{1,0:T(8,128)(2,1)S(1)}, bf16[128,256]{1,0:T(8,128)(2,1)S(1)}, u32[]{:S(2)}, u32[]{:S(2)}) %collective-permute-start.2) | collective-permute-done | bytes 65568 | tf_op jit(solution)/shard_map/ppermute | solution.py:13
  19.5 0.5 fusion.4
  20.3 16.9 %all-gather = f32[512,256]{0,1:T(8,128)S(1)} all-gather(f32[128,256]{0,1:T(8,128)S(1)} %fusion.10), channel_id=2, replica_groups=mesh['parts'=2,'leaf'=4,'top'=4] {'leaf'}, dimensions={0}, use_global_device_ids=true | all-gather | bytes 655360 | tf_op jit(solution)/shard_map/all_gather | solution.py:7
  37.7 5.9 %all_gather.20 = bf16[512,256]{0,1:T(8,128)(2,1)S(1)} all-gather(bf16[128,256]{0,1:T(8,128)(2,1)S(1)} %reduce_sum.18), channel_id=1, replica_groups=mesh['parts'=2,'leaf'=4,'top'=4] {'top'}, dimensions={0}, use_global_device_ids=true | all-gather | bytes 327680 | tf_op jit(solution)/shard_map/all_gather | solution.py:59
  43.7 0.6 fusion.3
  44.5 15.6 %all-gather.1 = f32[512,256]{0,1:T(8,128)S(1)} all-gather(f32[128,256]{0,1:T(8,128)S(1)} %fusion.9), channel_id=3, replica_groups=mesh['parts'=2,'leaf'=4,'top'=4] {'leaf'}, dimensions={0}, use_global_device_ids=true | all-gather | bytes 655360 | tf_op jit(solution)/shard_map/all_gather | solution.py:7
  60.7 5.9 %all_gather.23 = bf16[512,256]{0,1:T(8,128)(2,1)S(1)} all-gather(bf16[128,256]{0,1:T(8,128)(2,1)S(1)} %reduce_sum.19), channel_id=1, replica_groups=mesh['parts'=2,'leaf'=4,'top'=4] {'top'}, dimensions={0}, use_global_device_ids=true | all-gather | bytes 327680 | tf_op jit(solution)/shard_map/all_gather | solution.py:59
  66.6 0.6 fusion.2
  67.5 1.5 %collective-permute-start.3 = (f32[128,256]{1,0:T(8,128)S(1)}, f32[128,256]{1,0:T(8,128)S(1)}, u32[]{:S(2)}, u32[]{:S(2)}) collective-permute-start(f32[128,256]{1,0:T(8,128)S(1)} %fusion.8), channel_id=1, source_target_pairs={{0,4},{4,0},{8,12},{12,8},{1,5},{5,1},{9,13},{13,9},{2,6},{6,2},{1... | collective-permute-start | bytes 393224 | tf_op jit(solution)/shard_map/ppermute | solution.py:13
  69.0 4.3 %collective-permute-done.3 = f32[128,256]{1,0:T(8,128)S(1)} collective-permute-done((f32[128,256]{1,0:T(8,128)S(1)}, f32[128,256]{1,0:T(8,128)S(1)}, u32[]{:S(2)}, u32[]{:S(2)}) %collective-permute-start.3) | collective-permute-done | bytes 131104 | tf_op jit(solution)/shard_map/ppermute | solution.py:13
  73.3 2.3 %collective-permute-start.4 = (bf16[128,256]{1,0:T(8,128)(2,1)S(1)}, bf16[128,256]{1,0:T(8,128)(2,1)S(1)}, u32[]{:S(2)}, u32[]{:S(2)}) collective-permute-start(bf16[128,256]{1,0:T(8,128)(2,1)S(1)} %add.7), channel_id=1, source_target_pairs={{0,8},{4,12},{8,0},{12,4},{1,9},{5,13},{9,1},{13,5},{2,10},{6,14},... | collective-permute-start | bytes 196616 | tf_op jit(solution)/shard_map/ppermute | solution.py:13
  75.6 3.1 %collective-permute-done.4 = bf16[128,256]{1,0:T(8,128)(2,1)S(1)} collective-permute-done((bf16[128,256]{1,0:T(8,128)(2,1)S(1)}, bf16[128,256]{1,0:T(8,128)(2,1)S(1)}, u32[]{:S(2)}, u32[]{:S(2)}) %collective-permute-start.4) | collective-permute-done | bytes 65568 | tf_op jit(solution)/shard_map/ppermute | solution.py:13
  78.7 0.5 fusion.1
  79.5 1.3 %collective-permute-start.5 = (bf16[128,256]{1,0:T(8,128)(2,1)S(1)}, bf16[128,256]{1,0:T(8,128)(2,1)S(1)}, u32[]{:S(2)}, u32[]{:S(2)}) collective-permute-start(bf16[128,256]{1,0:T(8,128)(2,1)S(1)} %fusion.7), channel_id=1, source_target_pairs={{0,4},{4,0},{8,12},{12,8},{1,5},{5,1},{9,13},{13,9},{2,6},{6,2},{1... | collective-permute-start | bytes 196616 | tf_op jit(solution)/shard_map/ppermute | solution.py:13
  80.8 3.0 %collective-permute-done.5 = bf16[128,256]{1,0:T(8,128)(2,1)S(1)} collective-permute-done((bf16[128,256]{1,0:T(8,128)(2,1)S(1)}, bf16[128,256]{1,0:T(8,128)(2,1)S(1)}, u32[]{:S(2)}, u32[]{:S(2)}) %collective-permute-start.5) | collective-permute-done | bytes 65568 | tf_op jit(solution)/shard_map/ppermute | solution.py:13
  84.1 0.7 convolution_bitcast_fusion
  84.8 1.1 %copy.20 = f32[1,640,256]{2,1,0:T(8,128)} copy(f32[1,640,256]{1,2,0:T(8,128)S(1)} %convolution_bitcast_fusion) | data formatting | bytes 1310720 | tf_op jit(solution)/shard_map/broadcast_in_dim | solution.py:91
  (33 shorter events, 3.4 us)
Async XLA Ops:
  0.0 1.1 %copy-start = (bf16[1,640,640]{2,1,0:T(8,128)(2,1)S(1)}, bf16[1,640,640]{2,1,0:T(8,128)(2,1)}, u32[]{:S(2)}) copy-start(bf16[1,640,640]{2,1,0:T(8,128)(2,1)} %param.9) | copy-start | bytes 2457604
  0.0 2.7 %copy-start.1 = (bf16[2,1,640,128]{3,2,1,0:T(8,128)(2,1)S(1)}, bf16[2,1,640,128]{3,2,1,0:T(8,128)(2,1)}, u32[]{:S(2)}) copy-start(bf16[2,1,640,128]{3,2,1,0:T(8,128)(2,1)} %param.11) | copy-start | bytes 983044
  2.7 5.6 %copy-start.2 = (bf16[2,1,640,128]{3,2,1,0:T(8,128)(2,1)S(1)}, bf16[2,1,640,128]{3,2,1,0:T(8,128)(2,1)}, u32[]{:S(2)}) copy-start(bf16[2,1,640,128]{3,2,1,0:T(8,128)(2,1)} %param.10) | copy-start | bytes 983044
  2.7 5.6 %copy-start.8 = (bf16[2,1,128,256]{3,2,1,0:T(8,128)(2,1)S(1)}, bf16[2,1,128,256]{3,2,1,0:T(8,128)(2,1)}, u32[]{:S(2)}) copy-start(bf16[2,1,128,256]{3,2,1,0:T(8,128)(2,1)} %param.12) | copy-start | bytes 393220
  3.0 5.3 %collective-permute-start = (bf16[128,256]{1,0:T(8,128)(2,1)S(1)}, bf16[128,256]{1,0:T(8,128)(2,1)S(1)}, u32[]{:S(2)}, u32[]{:S(2)}) collective-permute-start(bf16[128,256]{1,0:T(8,128)(2,1)S(1)} %fusion.12), channel_id=1, source_target_pairs={{0,4},{4,0},{8,12},{12,8},{1,5},{5,1},{9,13},{13,9},{2,6},{6,2},{1... | collective-permute-start | bytes 196616 | tf_op jit(solution)/shard_map/ppermute | solution.py:13
  9.1 5.0 %collective-permute-start.1 = (f32[128,256]{1,0:T(8,128)S(1)}, f32[128,256]{1,0:T(8,128)S(1)}, u32[]{:S(2)}, u32[]{:S(2)}) collective-permute-start(f32[128,256]{1,0:T(8,128)S(1)} %fusion.11), channel_id=1, source_target_pairs={{0,4},{4,0},{8,12},{12,8},{1,5},{5,1},{9,13},{13,9},{2,6},{6,2},{1... | collective-permute-start | bytes 393224 | tf_op jit(solution)/shard_map/ppermute | solution.py:13
  14.1 5.3 %collective-permute-start.2 = (bf16[128,256]{1,0:T(8,128)(2,1)S(1)}, bf16[128,256]{1,0:T(8,128)(2,1)S(1)}, u32[]{:S(2)}, u32[]{:S(2)}) collective-permute-start(bf16[128,256]{1,0:T(8,128)(2,1)S(1)} %add.6), channel_id=1, source_target_pairs={{0,8},{4,12},{8,0},{12,4},{1,9},{5,13},{9,1},{13,5},{2,10},{6,14},... | collective-permute-start | bytes 196616 | tf_op jit(solution)/shard_map/ppermute | solution.py:13
  17.2 2.7 %copy-start.4 = (bf16[1,640,128]{2,1,0:T(8,128)(2,1)S(1)}, bf16[1,640,128]{2,1,0:T(8,128)(2,1)}, u32[]{:S(2)}) copy-start(bf16[1,640,128]{2,1,0:T(8,128)(2,1)} %param.14) | copy-start | bytes 491524
  37.7 6.0 %copy-start.3 = (bf16[1,640,128]{2,1,0:T(8,128)(2,1)S(1)}, bf16[1,640,128]{2,1,0:T(8,128)(2,1)}, u32[]{:S(2)}) copy-start(bf16[1,640,128]{2,1,0:T(8,128)(2,1)} %param.13) | copy-start | bytes 491524
  37.7 6.0 %copy-start.6 = (bf16[128,512]{1,0:T(8,128)(2,1)S(1)}, bf16[128,512]{1,0:T(8,128)(2,1)}, u32[]{:S(2)}) copy-start(bf16[128,512]{1,0:T(8,128)(2,1)} %param.15) | copy-start | bytes 393220
  60.7 6.0 %copy-start.5 = (bf16[1,640,128]{2,1,0:T(8,128)(2,1)S(1)}, bf16[1,640,128]{2,1,0:T(8,128)(2,1)}, u32[]{:S(2)}) copy-start(bf16[1,640,128]{2,1,0:T(8,128)(2,1)} %param.14) | copy-start | bytes 491524
  60.7 6.0 %copy-start.7 = (bf16[128,512]{1,0:T(8,128)(2,1)S(1)}, bf16[128,512]{1,0:T(8,128)(2,1)}, u32[]{:S(2)}) copy-start(bf16[128,512]{1,0:T(8,128)(2,1)} %param.15) | copy-start | bytes 393220
  67.5 11.3 %copy-start.9 = (bf16[2,1,128,256]{3,2,1,0:T(8,128)(2,1)S(1)}, bf16[2,1,128,256]{3,2,1,0:T(8,128)(2,1)}, u32[]{:S(2)}) copy-start(bf16[2,1,128,256]{3,2,1,0:T(8,128)(2,1)} %param.12) | copy-start | bytes 393220
  67.5 5.8 %collective-permute-start.3 = (f32[128,256]{1,0:T(8,128)S(1)}, f32[128,256]{1,0:T(8,128)S(1)}, u32[]{:S(2)}, u32[]{:S(2)}) collective-permute-start(f32[128,256]{1,0:T(8,128)S(1)} %fusion.8), channel_id=1, source_target_pairs={{0,4},{4,0},{8,12},{12,8},{1,5},{5,1},{9,13},{13,9},{2,6},{6,2},{1... | collective-permute-start | bytes 393224 | tf_op jit(solution)/shard_map/ppermute | solution.py:13
  73.3 5.4 %collective-permute-start.4 = (bf16[128,256]{1,0:T(8,128)(2,1)S(1)}, bf16[128,256]{1,0:T(8,128)(2,1)S(1)}, u32[]{:S(2)}, u32[]{:S(2)}) collective-permute-start(bf16[128,256]{1,0:T(8,128)(2,1)S(1)} %add.7), channel_id=1, source_target_pairs={{0,8},{4,12},{8,0},{12,4},{1,9},{5,13},{9,1},{13,5},{2,10},{6,14},... | collective-permute-start | bytes 196616 | tf_op jit(solution)/shard_map/ppermute | solution.py:13
  79.5 4.3 %collective-permute-start.5 = (bf16[128,256]{1,0:T(8,128)(2,1)S(1)}, bf16[128,256]{1,0:T(8,128)(2,1)S(1)}, u32[]{:S(2)}, u32[]{:S(2)}) collective-permute-start(bf16[128,256]{1,0:T(8,128)(2,1)S(1)} %fusion.7), channel_id=1, source_target_pairs={{0,4},{4,0},{8,12},{12,8},{1,5},{5,1},{9,13},{13,9},{2,6},{6,2},{1... | collective-permute-start | bytes 196616 | tf_op jit(solution)/shard_map/ppermute | solution.py:13
